TPU v7x, 256 devices: a whole 4x4x8 slice. The times are simulated.
256 devices in a mesh: blk: 8 (over z_lo, core), wide: 32 (over x, z_hi, y).
Axes of the slice: x: 4, y: 4, z: 8 (z_hi: 2, z_lo: 4; z = z_hi * 4 + z_lo), core: 2. Of those that a mesh axis runs over, the one named last changes fastest.
Arguments:
- surf_xyz: float32 [3, 131072], P(None, ('blk', 'wide')), may hold values from -5 to 5
- surf_disp: float32 [24, 131072], P(None, ('blk', 'wide')), may hold values from -12 to 12
- neighbours: int32 [4, 131072], P(None, ('blk', 'wide')), may hold values from 0 to 16383, as said below
- vol_xyz: float32 [3, 65536], P(None, ('blk', 'wide')), may hold values from -4 to 4
Outputs:
- displacement: float32 [24, 65536], P(None, ('blk', 'wide'))
Inputs may be any that keep to these rules, and one draw needn't show every extreme that they name: `neighbours`: column j names surface nodes of the same group of 16384 consecutive nodes as j, by their index within that group; every group is a renumbering of square patches of 16 x 16 nodes.
All inputs are finite; a program needn't handle non-finite values.
Results may differ from a plain program's by a relative error of at most 0.012.
The roundings to bfloat16 on the way count: a program that leaves them out, or rounds other values in their place, can miss the bound.
Values may be sent and summed in bfloat16 or wider, within the bound.
A program may use at most 64 MiB of HBM per device.

v0:
```python
import math
import jax
import jax.numpy as jnp
from jax import lax
from jax.sharding import PartitionSpec as P

tangent_floor = 0.04
core_radius = 0.04


def from_behind(shard, axis, by):
    peers = lax.axis_size(axis)
    return lax.ppermute(shard, axis, [(i, (i + by) % peers) for i in range(peers)])


def form_blocks(source_xyz, source_disp, links, node_xyz, node_disp):
    count = links.shape[1]
    cases = node_disp.shape[0] // 3
    tangent_one = jnp.take(source_xyz, links[0], axis=1) - jnp.take(source_xyz, links[1], axis=1)
    tangent_two = jnp.take(source_xyz, links[2], axis=1) - jnp.take(source_xyz, links[3], axis=1)
    change_one = (
        jnp.take(source_disp, links[0], axis=1) - jnp.take(source_disp, links[1], axis=1)
    ).reshape(cases, 3, count)
    change_two = (
        jnp.take(source_disp, links[2], axis=1) - jnp.take(source_disp, links[3], axis=1)
    ).reshape(cases, 3, count)
    length_one = (
        tangent_one[0] * tangent_one[0]
        + tangent_one[1] * tangent_one[1]
        + tangent_one[2] * tangent_one[2]
    )
    length_two = (
        tangent_two[0] * tangent_two[0]
        + tangent_two[1] * tangent_two[1]
        + tangent_two[2] * tangent_two[2]
    )
    scaled_one = tangent_one / (length_one + tangent_floor)
    scaled_two = tangent_two / (length_two + tangent_floor)
    linear = (
        change_one[:, :, None, :] * scaled_one[None, None, :, :]
        + change_two[:, :, None, :] * scaled_two[None, None, :, :]
    )
    moved = node_disp.reshape(cases, 3, count)
    offset = (
        linear[:, :, 0, :] * node_xyz[0]
        + linear[:, :, 1, :] * node_xyz[1]
        + linear[:, :, 2, :] * node_xyz[2]
    )
    blocks = jnp.concatenate([linear.reshape(cases, 9, count), moved - offset], axis=1)
    return blocks.reshape(cases * 12, count).astype(jnp.bfloat16)


def pair_weights(source_xyz, target_xyz):
    delta_x = source_xyz[0][:, None] - target_xyz[0][None, :]
    delta_y = source_xyz[1][:, None] - target_xyz[1][None, :]
    delta_z = source_xyz[2][:, None] - target_xyz[2][None, :]
    radius = delta_x * delta_x + delta_y * delta_y + delta_z * delta_z + core_radius
    return (1.0 / (radius * radius)).astype(jnp.bfloat16)


def finish(numerator, denominator, target_xyz):
    cases = numerator.shape[0] // 12
    count = numerator.shape[1]
    grouped = numerator.reshape(cases, 12, count)
    linear = grouped[:, :9].reshape(cases, 3, 3, count)
    moved = (
        linear[:, :, 0] * target_xyz[0]
        + linear[:, :, 1] * target_xyz[1]
        + linear[:, :, 2] * target_xyz[2]
        + grouped[:, 9:]
    )
    return (moved / denominator).reshape(cases * 3, count)


def accumulate(blocks, group_xyz, target_xyz, numerator, denominator):
    count = blocks.shape[1]
    width = math.gcd(1024, count)

    def one_piece(index, carry):
        partial_num, partial_den = carry
        start = index * width
        block_piece = lax.dynamic_slice_in_dim(blocks, start, width, 1)
        source_piece = lax.dynamic_slice_in_dim(group_xyz, start, width, 1)
        weights = pair_weights(source_piece, target_xyz)
        partial_num = partial_num + jnp.dot(
            block_piece, weights, preferred_element_type=jnp.float32
        )
        partial_den = partial_den + jnp.sum(weights.astype(jnp.float32), axis=0)
        return (partial_num, partial_den)

    return lax.fori_loop(0, count // width, one_piece, (numerator, denominator))


def on_device(surf_xyz, surf_disp, neighbours, vol_xyz):
    group_xyz, group_disp = (
        lax.all_gather(surf_xyz, "wide", axis=1, tiled=True),
        lax.all_gather(surf_disp, "wide", axis=1, tiled=True),
    )
    own_blocks = form_blocks(group_xyz, group_disp, neighbours, surf_xyz, surf_disp)
    blocks = lax.all_gather(own_blocks, "wide", axis=1, tiled=True)
    rows = blocks.shape[0]
    volume = vol_xyz.shape[1]
    groups = lax.axis_size("blk")
    visit_xyz = vol_xyz
    numerator = jnp.zeros((rows, volume), jnp.float32)
    denominator = jnp.zeros((volume,), jnp.float32)
    for step in range(groups):
        numerator, denominator = accumulate(blocks, group_xyz, visit_xyz, numerator, denominator)
        visit_xyz, numerator, denominator = from_behind(
            (visit_xyz, numerator, denominator), "blk", 1
        )
    return finish(numerator, denominator, vol_xyz)


def solution(mesh):
    in_specs = (
        P(None, ("blk", "wide")),
        P(None, ("blk", "wide")),
        P(None, ("blk", "wide")),
        P(None, ("blk", "wide")),
    )
    out_specs = P(None, ("blk", "wide"))
    return jax.shard_map(
        on_device, mesh=mesh, in_specs=in_specs, out_specs=out_specs, check_vma=False
    )
```

profile of v0, /device:TPU:2, one launch (start us, length us, event | category | flops | bytes accessed | tf_op | source)
XLA Modules:
  0.0 806.8 jit_solution(5151948245214430202)
XLA Ops:
  6.5 1.6 copy.76
  10.0 316.1 %all_gather.10 = f32[3,16384]{0,1:T(8,128)} all-gather(f32[3,512]{0,1:T(8,128)S(1)} %copy.80), channel_id=1, replica_groups=mesh['blk'=8,'wide'=32] {'wide'}, dimensions={1}, use_global_device_ids=true | all-gather | bytes 202752 | tf_op jit(solution)/shard_map/all_gather | solution.py:96
  326.1 4.4 gather_fusion.7
  330.6 4.4 gather_fusion.6
  335.3 4.4 gather_fusion.3
  339.8 4.4 gather_fusion.2
  344.5 4.4 gather_fusion.5
  349.0 4.4 gather_fusion.4
  353.7 4.4 gather_fusion.1
  358.2 4.4 gather_fusion
  363.9 5.5 copy.90
  369.3 97.1 %all-gather.5.cloned.1.call-done = bf16[96,16384]{1,0:T(8,128)(2,1)} async-done(((bf16[96,512]{1,0:T(8,128)(2,1)}), bf16[96,16384]{1,0:T(8,128)(2,1)}) %all-gather.5.cloned.1.call-update) | async-done | bytes 3145744 | tf_op jit(solution)/shard_map/all_gather | solution.py:100
  466.4 35.8 %while.128 = (s32[]{:T(128)}, f32[96,256]{1,0:T(8,128)S(1)}, f32[256]{0:T(256)S(1)}, bf16[96,16384]{1,0:T(8,128)(2,1)}, f32[3,16384]{1,0:T(4,128)S(1)}, /*index=...) while((s32[]{:T(128)}, f32[96,256]{1,0:T(8,128)S(1)}, ...), condition=%wide.region_2.5_spmd.clone, body=%wide.region_0.4_spmd.clone.sunk | while | flops 57196808 | bytes 458974 | solution.py:91
  471.5 1.6 convolution_add_fusion.23
  478.2 1.6 convolution_add_fusion.23
  484.9 1.6 convolution_add_fusion.23
  491.7 1.6 convolution_add_fusion.23
  503.2 5.0 collective-permute-done.2
  508.3 35.6 %while.121 = (s32[]{:T(128)}, f32[96,256]{1,0:T(8,128)S(1)}, f32[256]{0:T(256)S(1)}, bf16[96,16384]{1,0:T(8,128)(2,1)}, f32[3,16384]{1,0:T(4,128)S(1)}, /*index=...) while((s32[]{:T(128)}, f32[96,256]{1,0:T(8,128)S(1)}, ...), condition=%wide.region_5.8_spmd, body=%wide.region_3.7_spmd.sunk | while | flops 57171976 | bytes 458955 | solution.py:91
  544.3 5.5 collective-permute-done.5
  549.8 35.5 %while.122 = (s32[]{:T(128)}, f32[96,256]{1,0:T(8,128)S(1)}, f32[256]{0:T(256)S(1)}, bf16[96,16384]{1,0:T(8,128)(2,1)}, f32[3,16384]{1,0:T(4,128)S(1)}, /*index=...) while((s32[]{:T(128)}, f32[96,256]{1,0:T(8,128)S(1)}, ...), condition=%wide.region_8.11_spmd, body=%wide.region_6.10_spmd.sunk | while | flops 57171976 | bytes 458955 | solution.py:91
  585.7 5.7 collective-permute-done.8
  591.4 35.5 %while.123 = (s32[]{:T(128)}, f32[96,256]{1,0:T(8,128)S(1)}, f32[256]{0:T(256)S(1)}, bf16[96,16384]{1,0:T(8,128)(2,1)}, f32[3,16384]{1,0:T(4,128)S(1)}, /*index=...) while((s32[]{:T(128)}, f32[96,256]{1,0:T(8,128)S(1)}, ...), condition=%wide.region_11.14_spmd, body=%wide.region_9.13_spmd.sunk | while | flops 57171976 | bytes 458955 | solution.py:91
  627.2 5.7 collective-permute-done.11
  633.0 35.5 %while.124 = (s32[]{:T(128)}, f32[96,256]{1,0:T(8,128)S(1)}, f32[256]{0:T(256)S(1)}, bf16[96,16384]{1,0:T(8,128)(2,1)}, f32[3,16384]{1,0:T(4,128)S(1)}, /*index=...) while((s32[]{:T(128)}, f32[96,256]{1,0:T(8,128)S(1)}, ...), condition=%wide.region_14.17_spmd, body=%wide.region_12.16_spmd.sunk | while | flops 57171976 | bytes 458955 | solution.py:91
  668.8 5.7 collective-permute-done.14
  674.6 35.5 %while.125 = (s32[]{:T(128)}, f32[96,256]{1,0:T(8,128)S(1)}, f32[256]{0:T(256)S(1)}, bf16[96,16384]{1,0:T(8,128)(2,1)}, f32[3,16384]{1,0:T(4,128)S(1)}, /*index=...) while((s32[]{:T(128)}, f32[96,256]{1,0:T(8,128)S(1)}, ...), condition=%wide.region_17.20_spmd, body=%wide.region_15.19_spmd.sunk | while | flops 57171976 | bytes 458955 | solution.py:91
  710.6 5.5 collective-permute-done.17
  716.1 35.5 %while.126 = (s32[]{:T(128)}, f32[96,256]{1,0:T(8,128)S(1)}, f32[256]{0:T(256)S(1)}, bf16[96,16384]{1,0:T(8,128)(2,1)}, f32[3,16384]{1,0:T(4,128)S(1)}, /*index=...) while((s32[]{:T(128)}, f32[96,256]{1,0:T(8,128)S(1)}, ...), condition=%wide.region_20.23_spmd, body=%wide.region_18.22_spmd.sunk | while | flops 57171976 | bytes 458955 | solution.py:91
  752.0 5.7 collective-permute-done.20
  757.7 35.5 %while.127 = (s32[]{:T(128)}, f32[96,256]{1,0:T(8,128)S(1)}, f32[256]{0:T(256)S(1)}, bf16[96,16384]{1,0:T(8,128)(2,1)}, f32[3,16384]{1,0:T(4,128)S(1)}, /*index=...) while((s32[]{:T(128)}, f32[96,256]{1,0:T(8,128)S(1)}, ...), condition=%wide.region_23.26_spmd, body=%wide.region_21.25_spmd.sunk | while | flops 57171976 | bytes 458955 | solution.py:91
  793.5 5.7 collective-permute-done.21
  (735 shorter events, 281.0 us)
Async XLA Ops:
  6.5 338.0 %all-gather.3.cloned.1.call-start = ((), (), s32[]{:S(2)}) async-start(), calls=%async_computation | async-start | bytes 8650752 | tf_op jit(solution)/shard_map/all_gather | solution.py:97
  8.2 458.2 %all-gather.5.cloned.1.call-start = ((), (), s32[]{:S(2)}) async-start(), calls=%async_computation.1 | async-start | bytes 3244032 | tf_op jit(solution)/shard_map/all_gather | solution.py:100
  10.0 316.1 %copy-start = (f32[24,512]{1,0:T(8,128)S(1)}, f32[24,512]{1,0:T(8,128)}, u32[]{:S(2)}) copy-start(f32[24,512]{1,0:T(8,128)} %param.25) | copy-start | bytes 147460
  10.0 334.5 %copy-start.2 = (f32[3,512]{1,0:T(4,128)S(1)}, f32[3,512]{1,0:T(4,128)}, u32[]{:S(2)}) copy-start(f32[3,512]{1,0:T(4,128)} %param.24) | copy-start | bytes 18436
  363.8 102.6 %copy-start.1 = (f32[3,256]{1,0:T(4,128)S(1)}, f32[3,256]{1,0:T(4,128)}, u32[]{:S(2)}) copy-start(f32[3,256]{1,0:T(4,128)} %param.27) | copy-start | bytes 9220
  502.3 6.0 collective-permute-start
  502.3 5.9 collective-permute-start.2
  503.1 5.1 collective-permute-start.1
  543.8 6.0 collective-permute-start.3
  543.9 5.9 collective-permute-start.5
  544.0 5.8 collective-permute-start.4
  585.4 6.0 collective-permute-start.6
  585.5 5.9 collective-permute-start.8
  585.6 5.8 collective-permute-start.7
  627.0 6.0 collective-permute-start.9
  627.1 5.9 collective-permute-start.11
  627.2 5.8 collective-permute-start.10
  668.6 6.0 collective-permute-start.12
  668.6 5.9 collective-permute-start.14
  668.7 5.8 collective-permute-start.13
  710.1 6.0 collective-permute-start.15
  710.2 5.9 collective-permute-start.17
  710.5 5.6 collective-permute-start.16
  751.7 6.0 collective-permute-start.18
  751.8 5.9 collective-permute-start.20
  751.9 5.8 collective-permute-start.19
  793.3 5.9 collective-permute-start.21
  793.4 5.9 collective-permute-start.22
Sparse Core Ops, SparseCore 0:
  10.9 230.4 all-gather.2
  363.9 102.4 all-gather.4
where the time goes:
time: 811 us; the launch traced here: 807 us
  blocking collectives  316 us (39%)
  matrix products  201 us (25%)
  waiting for transfers between devices  142 us (18%)
  other arithmetic  66.2 us (8%)
  local copies, waits for them, and re-layouts  58.7 us (7%)
  between operations  14 us (2%)
    all_gather x1, blocking collectives, on_device(): lax.all_gather(surf_xyz, 'wide', axis=1, tiled=True)  316 us
    dot_general x128, matrix products, one_piece(): jnp.dot(block_piece, weights, preferred_element_type=jnp.float32)  201 us
    all_gather x1, waiting for transfers between devices, on_device(): blocks = lax.all_gather(own_blocks, 'wide', axis=1, tiled=True)  97.1 us
    reduce_sum x128, other arithmetic, one_piece(): partial_den = partial_den + jnp.sum(weights.astype(jnp.float32), axis=0)  64.1 us
    ppermute x23, waiting for transfers between devices, from_behind(): lax.ppermute(shard, axis, [(i, (i + by) % peers) for i in range(peers)])  44.8 us
  transfers between devices with their start and end apart: 25, of which 16 were waited for; matrix products, arithmetic and copies ran while one was open for 3% of the time, Pallas kernels for 0%

commit v1 on v0

--- a/solution.py
+++ b/solution.py
@@ -97,7 +97,8 @@
         lax.all_gather(surf_disp, "wide", axis=1, tiled=True),
     )
     own_blocks = form_blocks(group_xyz, group_disp, neighbours, surf_xyz, surf_disp)
-    blocks = lax.all_gather(own_blocks, "wide", axis=1, tiled=True)
+    sent = jnp.stack([own_blocks] * lax.axis_size("wide"))
+    blocks = jnp.concatenate(lax.all_to_all(sent, "wide", 0, 0), axis=1)
     rows = blocks.shape[0]
     volume = vol_xyz.shape[1]
     groups = lax.axis_size("blk")

time: 811 us -> 786 us (0.969)
  waiting for transfers between devices: 142 us -> 79.6 us
  starting transfers between devices: 3.08 us -> 38.6 us
    all_gather x1 -> x0, waiting for transfers between devices: 97.1 us -> none  [on_device(): blocks = lax.all_gather(own_blocks, 'wide', axis=1, tiled=True)]
    all_to_all x0 -> x1, waiting for transfers between devices: none -> 30.6 us  [on_device(): blocks = jnp.concatenate(lax.all_to_all(sent, 'wide', 0, 0), axis=1)]
    ppermute x23, starting transfers between devices: 3.04 us -> 33.4 us  [from_behind(): lax.ppermute(shard, axis, [(i, (i + by) % peers) for i in range(peers)])]
where the time goes in v1:
time: 786 us; the launch traced here: 780 us
  blocking collectives  313 us (40%)
  matrix products  201 us (26%)
  waiting for transfers between devices  79.6 us (10%)
  other arithmetic  66.2 us (8%)
  local copies, waits for them, and re-layouts  62 us (8%)
  starting transfers between devices  38.6 us (5%)
  between operations  14 us (2%)
    all_gather x1, blocking collectives, on_device(): lax.all_gather(surf_xyz, 'wide', axis=1, tiled=True)  313 us
    dot_general x128, matrix products, one_piece(): jnp.dot(block_piece, weights, preferred_element_type=jnp.float32)  201 us
    reduce_sum x128, other arithmetic, one_piece(): partial_den = partial_den + jnp.sum(weights.astype(jnp.float32), axis=0)  64.1 us
    ppermute x23, waiting for transfers between devices, from_behind(): lax.ppermute(shard, axis, [(i, (i + by) % peers) for i in range(peers)])  49 us
    ppermute x23, starting transfers between devices, from_behind(): lax.ppermute(shard, axis, [(i, (i + by) % peers) for i in range(peers)])  33.4 us
    all_to_all x1, waiting for transfers between devices, on_device(): blocks = jnp.concatenate(lax.all_to_all(sent, 'wide', 0, 0), axis=1)  30.6 us
  transfers between devices with their start and end apart: 25, of which 16 were waited for; matrix products, arithmetic and copies ran while one was open for 3% of the time, Pallas kernels for 0%

profile of v1, /device:TPU:2, one launch (start us, length us, event | category | flops | bytes accessed | tf_op | source)
XLA Modules:
  0.0 780.2 jit_solution(4097525712431516913)
XLA Ops:
  9.9 313.0 %all_gather.7 = f32[3,16384]{0,1:T(8,128)} all-gather(f32[3,512]{0,1:T(8,128)S(1)} %copy.134), channel_id=1, replica_groups=mesh['blk'=8,'wide'=32] {'wide'}, dimensions={1}, use_global_device_ids=true | all-gather | bytes 202752 | tf_op jit(solution)/shard_map/all_gather | solution.py:96
  322.9 4.4 gather_fusion.7
  327.5 4.4 gather_fusion.6
  332.2 4.4 gather_fusion.3
  336.7 4.4 gather_fusion.2
  341.4 4.4 gather_fusion.5
  345.8 4.4 gather_fusion.4
  350.6 4.4 gather_fusion.1
  355.0 4.4 gather_fusion
  362.0 5.2 all-to-all-start
  367.2 5.5 copy.145
  372.7 30.6 %all-to-all-done = bf16[32,96,512]{2,1,0:T(8,128)(2,1)S(1)} async-done(((bf16[32,96,512]{2,1,0:T(8,128)(2,1)}), bf16[32,96,512]{2,1,0:T(8,128)(2,1)S(1)}, u32[]{:S(2)}, u32[]{:S(2)}) %all-to-all-start) | async-done | bytes 3145760 | tf_op jit(solution)/shard_map/all_to_all | solution.py:101
  405.2 35.8 %while.128 = (s32[]{:T(128)}, f32[96,256]{1,0:T(8,128)S(1)}, f32[256]{0:T(256)S(1)}, bf16[96,16384]{1,0:T(8,128)(2,1)}, f32[3,16384]{1,0:T(4,128)S(1)}, /*index=...) while((s32[]{:T(128)}, f32[96,256]{1,0:T(8,128)S(1)}, ...), condition=%wide.region_2.5_spmd.clone, body=%wide.region_0.4_spmd.clone.sunk | while | flops 57196808 | bytes 458974 | solution.py:91
  441.2 22.8 %collective-permute-start.2 = (f32[3,256]{1,0:T(4,128)S(1)}, f32[3,256]{1,0:T(4,128)S(1)}, u32[]{:S(2)}, u32[]{:S(2)}) collective-permute-start(f32[3,256]{1,0:T(4,128)S(1)} %get-tuple-element.2075), channel_id=1, source_target_pairs={{0,32},{32,64},{64,96},{96,128},{128,160},{160,192},{192,224},{224... | collective-permute-start | bytes 9224 | tf_op jit(solution)/shard_map/ppermute | solution.py:13
  464.1 10.0 %collective-permute-done.2 = f32[3,256]{1,0:T(4,128)S(1)} collective-permute-done((f32[3,256]{1,0:T(4,128)S(1)}, f32[3,256]{1,0:T(4,128)S(1)}, u32[]{:S(2)}, u32[]{:S(2)}) %collective-permute-start.2) | collective-permute-done | bytes 3104 | tf_op jit(solution)/shard_map/ppermute | solution.py:13
  474.1 35.5 %while.121 = (s32[]{:T(128)}, f32[96,256]{1,0:T(8,128)S(1)}, f32[256]{0:T(256)S(1)}, bf16[96,16384]{1,0:T(8,128)(2,1)}, f32[3,16384]{1,0:T(4,128)S(1)}, /*index=...) while((s32[]{:T(128)}, f32[96,256]{1,0:T(8,128)S(1)}, ...), condition=%wide.region_5.8_spmd, body=%wide.region_3.7_spmd.sunk | while | flops 57171976 | bytes 458955 | solution.py:91
  509.7 6.5 collective-permute-start.3
  516.2 2.3 collective-permute-start.5
  518.5 2.5 collective-permute-done.5
  521.0 2.3 collective-permute-done.4
  523.2 35.6 %while.122 = (s32[]{:T(128)}, f32[96,256]{1,0:T(8,128)S(1)}, f32[256]{0:T(256)S(1)}, bf16[96,16384]{1,0:T(8,128)(2,1)}, f32[3,16384]{1,0:T(4,128)S(1)}, /*index=...) while((s32[]{:T(128)}, f32[96,256]{1,0:T(8,128)S(1)}, ...), condition=%wide.region_8.11_spmd, body=%wide.region_6.10_spmd.sunk | while | flops 57171976 | bytes 458955 | solution.py:91
  559.1 5.7 collective-permute-done.8
  564.8 35.5 %while.123 = (s32[]{:T(128)}, f32[96,256]{1,0:T(8,128)S(1)}, f32[256]{0:T(256)S(1)}, bf16[96,16384]{1,0:T(8,128)(2,1)}, f32[3,16384]{1,0:T(4,128)S(1)}, /*index=...) while((s32[]{:T(128)}, f32[96,256]{1,0:T(8,128)S(1)}, ...), condition=%wide.region_11.14_spmd, body=%wide.region_9.13_spmd.sunk | while | flops 57171976 | bytes 458955 | solution.py:91
  600.6 5.7 collective-permute-done.11
  606.4 35.5 %while.124 = (s32[]{:T(128)}, f32[96,256]{1,0:T(8,128)S(1)}, f32[256]{0:T(256)S(1)}, bf16[96,16384]{1,0:T(8,128)(2,1)}, f32[3,16384]{1,0:T(4,128)S(1)}, /*index=...) while((s32[]{:T(128)}, f32[96,256]{1,0:T(8,128)S(1)}, ...), condition=%wide.region_14.17_spmd, body=%wide.region_12.16_spmd.sunk | while | flops 57171976 | bytes 458955 | solution.py:91
  642.2 5.7 collective-permute-done.14
  648.0 35.5 %while.125 = (s32[]{:T(128)}, f32[96,256]{1,0:T(8,128)S(1)}, f32[256]{0:T(256)S(1)}, bf16[96,16384]{1,0:T(8,128)(2,1)}, f32[3,16384]{1,0:T(4,128)S(1)}, /*index=...) while((s32[]{:T(128)}, f32[96,256]{1,0:T(8,128)S(1)}, ...), condition=%wide.region_17.20_spmd, body=%wide.region_15.19_spmd.sunk | while | flops 57171976 | bytes 458955 | solution.py:91
  684.0 5.5 collective-permute-done.17
  689.5 35.5 %while.126 = (s32[]{:T(128)}, f32[96,256]{1,0:T(8,128)S(1)}, f32[256]{0:T(256)S(1)}, bf16[96,16384]{1,0:T(8,128)(2,1)}, f32[3,16384]{1,0:T(4,128)S(1)}, /*index=...) while((s32[]{:T(128)}, f32[96,256]{1,0:T(8,128)S(1)}, ...), condition=%wide.region_20.23_spmd, body=%wide.region_18.22_spmd.sunk | while | flops 57171976 | bytes 458955 | solution.py:91
  725.4 5.7 collective-permute-done.20
  731.1 35.5 %while.127 = (s32[]{:T(128)}, f32[96,256]{1,0:T(8,128)S(1)}, f32[256]{0:T(256)S(1)}, bf16[96,16384]{1,0:T(8,128)(2,1)}, f32[3,16384]{1,0:T(4,128)S(1)}, /*index=...) while((s32[]{:T(128)}, f32[96,256]{1,0:T(8,128)S(1)}, ...), condition=%wide.region_23.26_spmd, body=%wide.region_21.25_spmd.sunk | while | flops 57171976 | bytes 458955 | solution.py:91
  766.9 5.7 collective-permute-done.21
  (736 shorter events, 291.0 us)
Async XLA Ops:
  6.5 334.9 %all-gather.2.cloned.1.call-start = ((), (), s32[]{:S(2)}) async-start(), calls=%async_computation.1 | async-start | bytes 8650752 | tf_op jit(solution)/shard_map/all_gather | solution.py:97
  9.9 313.0 %copy-start = (f32[24,512]{1,0:T(8,128)S(1)}, f32[24,512]{1,0:T(8,128)}, u32[]{:S(2)}) copy-start(f32[24,512]{1,0:T(8,128)} %param.25) | copy-start | bytes 147460
  9.9 331.4 %copy-start.2 = (f32[3,512]{1,0:T(4,128)S(1)}, f32[3,512]{1,0:T(4,128)}, u32[]{:S(2)}) copy-start(f32[3,512]{1,0:T(4,128)} %param.24) | copy-start | bytes 18436
  362.0 41.2 %all-to-all-start = ((bf16[32,96,512]{2,1,0:T(8,128)(2,1)}), bf16[32,96,512]{2,1,0:T(8,128)(2,1)S(1)}, u32[]{:S(2)}, u32[]{:S(2)}) async-start(bf16[32,96,512]{2,1,0:T(8,128)(2,1)} %stack.2), calls=%async_computation | async-start | bytes 6291456 | tf_op jit(solution)/shard_map/all_to_all | solution.py:101
  403.3 2.0 copy-start.1
  441.1 33.1 %collective-permute-start = (f32[96,256]{1,0:T(8,128)S(1)}, f32[96,256]{1,0:T(8,128)S(1)}, u32[]{:S(2)}, u32[]{:S(2)}) collective-permute-start(f32[96,256]{1,0:T(8,128)S(1)} %get-tuple-element.887), channel_id=1, source_target_pairs={{0,32},{32,64},{64,96},{96,128},{128,160},{160,192},{192,224},{224... | collective-permute-start | bytes 294920 | tf_op jit(solution)/shard_map/ppermute | solution.py:13
  441.2 32.9 %collective-permute-start.2 = (f32[3,256]{1,0:T(4,128)S(1)}, f32[3,256]{1,0:T(4,128)S(1)}, u32[]{:S(2)}, u32[]{:S(2)}) collective-permute-start(f32[3,256]{1,0:T(4,128)S(1)} %get-tuple-element.2075), channel_id=1, source_target_pairs={{0,32},{32,64},{64,96},{96,128},{128,160},{160,192},{192,224},{224... | collective-permute-start | bytes 9224 | tf_op jit(solution)/shard_map/ppermute | solution.py:13
  464.0 10.2 %collective-permute-start.1 = (f32[256]{0:T(256)S(1)}, f32[256]{0:T(256)S(1)}, u32[]{:S(2)}, u32[]{:S(2)}) collective-permute-start(f32[256]{0:T(256)S(1)} %get-tuple-element.888), channel_id=1, source_target_pairs={{0,32},{32,64},{64,96},{96,128},{128,160},{160,192},{192,224},{224... | collective-permute-start | bytes 3080 | tf_op jit(solution)/shard_map/ppermute | solution.py:13
  509.7 13.5 %collective-permute-start.3 = (f32[96,256]{1,0:T(8,128)S(1)}, f32[96,256]{1,0:T(8,128)S(1)}, u32[]{:S(2)}, u32[]{:S(2)}) collective-permute-start(f32[96,256]{1,0:T(8,128)S(1)} %get-tuple-element.889), channel_id=1, source_target_pairs={{0,32},{32,64},{64,96},{96,128},{128,160},{160,192},{192,224},{224... | collective-permute-start | bytes 294920 | tf_op jit(solution)/shard_map/ppermute | solution.py:13
  516.2 4.8 collective-permute-start.5
  518.4 4.8 collective-permute-start.4
  558.8 6.0 collective-permute-start.6
  558.9 5.9 collective-permute-start.8
  559.0 5.8 collective-permute-start.7
  600.4 6.0 collective-permute-start.9
  600.5 5.9 collective-permute-start.11
  600.6 5.8 collective-permute-start.10
  641.9 6.0 collective-permute-start.12
  642.0 5.9 collective-permute-start.14
  642.1 5.8 collective-permute-start.13
  683.5 6.0 collective-permute-start.15
  683.6 5.9 collective-permute-start.17
  683.9 5.6 collective-permute-start.16
  725.1 6.0 collective-permute-start.18
  725.2 5.9 collective-permute-start.20
  725.3 5.8 collective-permute-start.19
  766.7 5.9 collective-permute-start.21
  766.8 5.9 collective-permute-start.22
Sparse Core Ops, SparseCore 0:
  10.9 223.8 all-gather.1
